TPU v7x, 256 devices: a whole 4x4x8 slice. The times are simulated.
256 devices in a mesh: dp: 32 (over z_lo, x, core), tensor: 8 (over y, z_hi).
Axes of the slice: x: 4, y: 4, z: 8 (z_hi: 2, z_lo: 4; z = z_hi * 4 + z_lo), core: 2. Of those that a mesh axis runs over, the one named last changes fastest.
Arguments:
- hidden: bfloat16 [32768, 28672], P('dp', 'tensor'), may hold values from -6 to 6
- out_grad: bfloat16 [32768, 8192], P('dp', 'tensor'), may hold values from -6 to 6
- proj_in: bfloat16 [28672, 64], P('tensor'), may hold values from -0.03125 to 0.03125
- proj_out: bfloat16 [8192, 64], P('tensor'), may hold values from -0.0625 to 0.0625
- owner_ids: int32 [32768, 1], P('dp'), may hold values from 0 to 31; in each aligned block of 1024 rows (0 to 1023, 1024 to 2047, ...) at most 128 rows name the same one
- example_ids: int32 [32768], P('dp'), may hold values from 0 to 127
Outputs:
- kernel: float32 [4096, 4096], P('tensor', 'dp')
Inputs may be any that keep to these rules, and one draw needn't show every extreme that they name: `owner_ids`: among the rows of one index of dp, at most 128 name the same owner, and every draw reaches 128.
All inputs are finite; a program needn't handle non-finite values.
Results may differ from a plain program's by a relative error of at most 0.009.
Values may be sent and summed in bfloat16 or wider, within the bound.
A program may use at most 64 MiB of HBM per device.

v0:
```python
import jax
import jax.numpy as jnp
from jax import lax
from jax.sharding import PartitionSpec as P

EX_DEV = 128


def outer_rows(x_rows, g_rows):
    return (x_rows[:, :, None] * g_rows[:, None, :]).reshape(
        x_rows.shape[0], x_rows.shape[1] * g_rows.shape[1]
    )


def member_dot(member, outer):
    member_half = member.astype(jnp.bfloat16)
    upper = outer.astype(jnp.bfloat16)
    lower = (outer - upper.astype(jnp.float32)).astype(jnp.bfloat16)
    first = jnp.dot(member_half, upper, preferred_element_type=jnp.float32)
    return first + jnp.dot(member_half, lower, preferred_element_type=jnp.float32)


def body(hidden, out_grad, proj_in, proj_out, owner_ids, example_ids):
    tensors = lax.axis_size("tensor")
    trank = lax.axis_index("tensor")
    groups = lax.axis_size("dp")
    width = proj_in.shape[1]
    share = width // tensors
    tok = hidden.shape[0]
    x_part = jnp.dot(hidden, proj_in, preferred_element_type=jnp.float32)
    g_part = jnp.dot(out_grad, proj_out, preferred_element_type=jnp.float32)
    send_rows = lax.psum(jnp.concatenate([x_part, g_part], 1), "tensor")
    x_start = trank * share
    columns = send_rows.shape[1]
    owners = owner_ids[:, 0]
    capacity = 4 * tok // groups
    owner_hot = (owners[:, None] == jnp.arange(groups, dtype=jnp.int32)[None, :]).astype(jnp.int32)
    slot_index = jnp.sum(jnp.cumsum(owner_hot, 0) * owner_hot, 1) - 1
    target = owners * capacity + slot_index
    row_buffer = jnp.zeros((groups * capacity, columns), jnp.float32).at[target].set(send_rows)
    id_buffer = (
        jnp.full((groups * capacity,), -1.0, jnp.float32)
        .at[target]
        .set(example_ids.astype(jnp.float32))
    )
    got_rows, got_ids = (
        lax.all_to_all(
            row_buffer.reshape(groups, capacity, columns),
            "dp",
            split_axis=0,
            concat_axis=0,
            tiled=True,
        ),
        lax.all_to_all(
            id_buffer.reshape(groups, capacity), "dp", split_axis=0, concat_axis=0, tiled=True
        ),
    )
    rows = got_rows.reshape(groups * capacity, columns)
    x_rows = lax.dynamic_slice_in_dim(rows, x_start, share, 1)
    g_rows = rows[:, columns - width :]
    member = (
        got_ids.reshape(1, groups * capacity) == jnp.arange(EX_DEV, dtype=jnp.float32)[:, None]
    ).astype(jnp.float32)
    sums = member_dot(member, outer_rows(x_rows, g_rows))
    counts = jnp.sum(member, 1)
    grads = (sums / jnp.maximum(counts, 1.0)[:, None]).astype(jnp.bfloat16)
    products = (
        lax.dot_general(
            lax.all_gather(grads, "dp", axis=0, tiled=True),
            grads,
            (((1,), (1,)), ((), ())),
            preferred_element_type=jnp.float32,
        )
        / width
    )
    return lax.psum_scatter(products, "tensor", scatter_dimension=0, tiled=True)


def solution(mesh):
    in_specs = (
        P("dp", "tensor"),
        P("dp", "tensor"),
        P("tensor", None),
        P("tensor", None),
        P("dp", None),
        P("dp"),
    )
    out_specs = P("tensor", "dp")
    return jax.shard_map(body, mesh=mesh, in_specs=in_specs, out_specs=out_specs, check_vma=False)
```

profile of v0, /device:TPU:21, one launch (start us, length us, event | category | flops | bytes accessed | tf_op | source)
XLA Modules:
  0.0 373.6 jit_solution(12380154530716794183)
XLA Ops:
  6.5 5.6 %fusion.15 = f32[1024,64]{0,1:T(8,128)S(1)} fusion(bf16[1024,3584]{1,0:T(8,128)(2,1)} %param.6, bf16[3584,64]{0,1:T(8,128)(2,1)} %param.8), kind=kOutput, calls=%fused_computation.33 | convolution fusion | flops 469762048 | bytes 8060928 | tf_op jit(solution)/shard_map/dot_general | solution.py:30
  12.1 0.8 fusion.16
  12.9 0.9 pad_maximum_fusion
  13.8 0.0 all-reduce.2.cloned.1.call-update
  13.8 9.0 %reduce-window.6 = s32[32,8,128]{2,1,0:T(8,128)S(1)} reduce-window(s32[32,8,128]{2,1,0:T(8,128)S(1)} %fusion.12, s32[]{:T(128)} %constant.12.clone.1), window={size=1x1x128 pad=0_0x0_0x127_0}, to_apply=%region_0.0 | reduce-window | flops 4161536 | bytes 262148 | tf_op jit(solution)/shard_map/reduce-window
  22.8 0.1 slice.12
  22.9 0.1 copy.12
  23.1 0.1 copy.13
  23.2 0.1 broadcast_add_fusion
  23.4 4.9 %scatter_custom_fusion = f32[4096]{0:T(1024)} fusion(s32[1024]{0:T(1024)S(1)} %bitcast.45, f32[1024]{0:T(1024)S(1)} %convert_element_type.27, f32[]{:T(128)} %constant.10.clone.1), kind=kCustom, calls=%fused_computation.28 | custom fusion | bytes 16388 | tf_op jit(solution)/shard_map/scatter | solution.py:44
  28.3 9.3 %all-to-all-start = ((f32[32,1,128]{2,1,0:T(1,128)}), f32[32,1,128]{2,1,0:T(1,128)S(1)}, u32[]{:S(2)}, u32[]{:S(2)}) async-start(f32[32,1,128]{2,1,0:T(1,128)} %bitcast.6), calls=%async_computation | async-start | bytes 32768 | tf_op jit(solution)/shard_map/all_to_all | solution.py:54
  37.6 85.1 %all-reduce.2.cloned.1.call-done = f32[1024,128]{0,1:T(8,128)} async-done(((f32[1024,128]{0,1:T(8,128)}), f32[1024,128]{0,1:T(8,128)}) %all-reduce.2.cloned.1.call-update) | async-done | bytes 524304 | tf_op jit(solution)/shard_map/psum | solution.py:32
  122.8 1.2 copy.14
  124.0 4.5 %scatter_custom_fusion.1 = f32[4096,128]{1,0:T(8,128)} fusion(s32[1024]{0:T(1024)S(1)} %bitcast.46, f32[1024,128]{1,0:T(8,128)S(1)} %copy.14, f32[]{:T(128)} %constant.6.clone.1), kind=kCustom, calls=%fused_computation.15 | custom fusion | bytes 2097156 | tf_op jit(solution)/shard_map/scatter | solution.py:40
  128.5 9.5 %all-to-all-start.1 = ((f32[32,128,128]{2,1,0:T(8,128)}), f32[32,128,128]{2,1,0:T(8,128)}, u32[]{:S(2)}, u32[]{:S(2)}) async-start(f32[32,128,128]{2,1,0:T(8,128)} %bitcast.36), calls=%async_computation.1 | async-start | bytes 4194304 | tf_op jit(solution)/shard_map/all_to_all | solution.py:47
  138.0 0.0 all-gather.2.cloned.1.call-start
  138.0 0.3 convert_reduce_fusion
  138.3 47.6 %all-to-all-done.1 = f32[32,128,128]{2,1,0:T(8,128)} async-done(((f32[32,128,128]{2,1,0:T(8,128)}), f32[32,128,128]{2,1,0:T(8,128)}, u32[]{:S(2)}, u32[]{:S(2)}) %all-to-all-start.1) | async-done | bytes 2097184 | tf_op jit(solution)/shard_map/all_to_all | solution.py:47
  185.9 3.5 slice.14
  189.4 3.5 constant_dynamic-slice_fusion
  192.9 2.2 copy.17
  195.1 2.2 copy.18
  197.3 1.0 broadcast_multiply_fusion
  198.3 4.7 %fusion = (bf16[4096,512]{0,1:T(8,128)(2,1)}, bf16[4096,512]{0,1:T(8,128)(2,1)}) fusion(f32[4096,8,64]{0,2,1:T(8,128)S(1)} %broadcast_multiply_fusion), kind=kLoop, calls=%fused_computation.4 | loop fusion | flops 8388608 | bytes 16777216 | tf_op jit(solution)/shard_map/convert_element_type | solution.py:18
  203.0 3.8 %fusion.1 = f32[128,512]{1,0:T(8,128)S(1)} fusion(bf16[4096,512]{0,1:T(8,128)(2,1)} %get-tuple-element.5, f32[4096]{0:T(1024)S(1)} %bitcast.39), kind=kOutput, calls=%fused_computation.10 | convolution fusion | flops 538443776 | bytes 4472832 | tf_op jit(solution)/shard_map/dot_general | solution.py:20
  206.9 2.2 fusion.5
  209.1 0.0 all-gather.2.cloned.1.call-update
  209.1 0.0 reduce-scatter.2.cloned.1.call-start
  209.2 61.2 %all-gather.2.cloned.1.call-done = bf16[4096,512]{1,0:T(8,128)(2,1)} async-done(((bf16[128,512]{1,0:T(8,128)(2,1)}), bf16[4096,512]{1,0:T(8,128)(2,1)}) %all-gather.2.cloned.1.call-update) | async-done | bytes 4194320 | tf_op jit(solution)/shard_map/all_gather | solution.py:69
  270.3 4.8 %convolution_multiply_fusion = f32[4096,128]{1,0:T(8,128)} fusion(bf16[4096,512]{1,0:T(8,128)(2,1)} %all-gather.2.cloned.1.call-done, bf16[128,512]{1,0:T(8,128)(2,1)} %fusion.5), kind=kOutput, calls=%fused_computation.5 | convolution fusion | flops 537395200 | bytes 6422528 | tf_op jit(solution)/shard_map/dot_general | solution.py:68
  275.1 0.0 reduce-scatter.2.cloned.1.call-update
  275.1 91.9 %reduce-scatter.2.cloned.1.call-done = f32[512,128]{1,0:T(8,128)} async-done(((f32[4096,128]{1,0:T(8,128)}), f32[512,128]{1,0:T(8,128)}) %reduce-scatter.2.cloned.1.call-update) | async-done | bytes 262160 | tf_op jit(solution)/shard_map/reduce_scatter | solution.py:76
  (20 shorter events, 0.1 us)
Async XLA Ops:
  6.5 5.6 %copy-start = (bf16[1024,1024]{1,0:T(8,128)(2,1)S(1)}, bf16[1024,1024]{1,0:T(8,128)(2,1)}, u32[]{:S(2)}) copy-start(bf16[1024,1024]{1,0:T(8,128)(2,1)} %param.7) | copy-start | bytes 6291460
  6.5 5.6 %copy-start.2 = (bf16[1024,64]{0,1:T(8,128)(2,1)S(1)}, bf16[1024,64]{0,1:T(8,128)(2,1)}, u32[]{:S(2)}) copy-start(bf16[1024,64]{0,1:T(8,128)(2,1)} %param.9) | copy-start | bytes 393220
  6.5 116.2 %all-reduce.2.cloned.1.call-start = ((), (), s32[]{:S(2)}) async-start(), calls=%async_computation.3 | async-start | bytes 1048576 | tf_op jit(solution)/shard_map/psum | solution.py:32
  12.1 1.7 copy-start.3
  12.1 11.2 %copy-start.4 = (s32[1024]{0:T(1024)S(1)}, s32[1024]{0:T(1024)}, u32[]{:S(2)}) copy-start(s32[1024]{0:T(1024)} %param.11) | copy-start | bytes 12292
  28.3 100.2 %all-to-all-start = ((f32[32,1,128]{2,1,0:T(1,128)}), f32[32,1,128]{2,1,0:T(1,128)S(1)}, u32[]{:S(2)}, u32[]{:S(2)}) async-start(f32[32,1,128]{2,1,0:T(1,128)} %bitcast.6), calls=%async_computation | async-start | bytes 32768 | tf_op jit(solution)/shard_map/all_to_all | solution.py:54
  128.5 57.5 %all-to-all-start.1 = ((f32[32,128,128]{2,1,0:T(8,128)}), f32[32,128,128]{2,1,0:T(8,128)}, u32[]{:S(2)}, u32[]{:S(2)}) async-start(f32[32,128,128]{2,1,0:T(8,128)} %bitcast.36), calls=%async_computation.1 | async-start | bytes 4194304 | tf_op jit(solution)/shard_map/all_to_all | solution.py:47
  138.0 132.4 %all-gather.2.cloned.1.call-start = ((), (), s32[]{:S(2)}) async-start(), calls=%async_computation.4 | async-start | bytes 4325376 | tf_op jit(solution)/shard_map/all_gather | solution.py:69
  203.0 3.9 %copy-start.1 = (bf16[4096,512]{0,1:T(8,128)(2,1)S(1)}, bf16[4096,512]{0,1:T(8,128)(2,1)}, u32[]{:S(2)}) copy-start(bf16[4096,512]{0,1:T(8,128)(2,1)} %get-tuple-element.6) | copy-start | bytes 12582916
  209.1 157.9 %reduce-scatter.2.cloned.1.call-start = ((), (), s32[]{:S(2)}) async-start(), calls=%async_computation.5 | async-start | bytes 2359296 | tf_op jit(solution)/shard_map/reduce_scatter | solution.py:76
Sparse Core Ops, SparseCore 0:
  13.9 108.7 all-reduce.1
  209.2 61.0 all-gather.1
  275.2 91.7 reduce-scatter.1
where the time goes:
time: 377 us; the launch traced here: 374 us
  waiting for transfers between devices  286 us (76%)
  local copies, waits for them, and re-layouts  22.3 us (6%)
  starting transfers between devices  18.9 us (5%)
  matrix products  17.1 us (5%)
  other arithmetic  16.1 us (4%)
  between operations  13.3 us (4%)
    reduce_scatter x1, waiting for transfers between devices, body(): return lax.psum_scatter(products, 'tensor', scatter_dimension=0, tiled=True)  91.9 us
    psum x1, waiting for transfers between devices, body(): send_rows = lax.psum(jnp.concatenate([x_part, g_part], 1), 'tensor')  85.1 us
    all_gather x1, waiting for transfers between devices, body(): lax.all_gather(grads, 'dp', axis=0, tiled=True)  61.2 us
    all_to_all x1, waiting for transfers between devices, body(): lax.all_to_all(row_buffer.reshape(groups, capacity, columns), 'dp', split...  47.6 us
    all_to_all x1, starting transfers between devices, body(): lax.all_to_all(row_buffer.reshape(groups, capacity, columns), 'dp', split...  9.49 us
    all_to_all x1, starting transfers between devices, body(): lax.all_to_all(id_buffer.reshape(groups, capacity), 'dp', split_axis=0, c...  9.34 us
    another operation x3, other arithmetic  9.15 us
  transfers between devices with their start and end apart: 5, of which 4 were waited for; matrix products, arithmetic and copies ran while one was open for 5% of the time, Pallas kernels for 0%

commit v1 on v0

v1 whole, which is shorter than its diff:
```python
import jax
import jax.numpy as jnp
from jax import lax
from jax.experimental import pallas as pl
from jax.experimental.pallas import tpu as pltpu
from jax.sharding import PartitionSpec as P

TOK = 1024
PART = 256
EX = 128
R = 64
HALF = 32
COLS = HALF * HALF
GROUP = 4
NT = (((1,), (1,)), ((), ()))
MESH = pl.DeviceIdType.MESH
BF = jnp.bfloat16
F32 = jnp.float32


def nt(a, b):
    return lax.dot_general(a, b, NT, preferred_element_type=F32)


def kernel(
    hid, og, pin, pout, own, exi, out,
    hbuf, gbuf, pinb, poutb, part_own, rs_send, rs_recv, z_send, z_recv, vals, slots,
    ids_send, ids_recv, sbuf, rbuf, outer, member, acc, bbuf, abuf, keep, c_send, c_recv,
    hsem, gsem, psem, rs_ss, rs_rs, z_sem, v_ss, v_rs, i_ss, i_rs, t_ss, t_rs,
    a_ss, a_rs, x_ss, x_rs, b_ss, b_rs, c_ss, c_rs,
):
    dp = lax.axis_index("dp")
    tn = lax.axis_index("tensor")
    y = tn // 2
    zh = lax.rem(tn, 2)
    zl = dp // 8
    x = lax.rem(dp // 2, 4)
    core = lax.rem(dp, 2)

    def remote(src, dst, ss, rs, **where):
        return pltpu.make_async_remote_copy(
            src_ref=src, dst_ref=dst, send_sem=ss, recv_sem=rs,
            device_id=where, device_id_type=MESH,
        )

    def at_y(k):
        return lax.rem(y + k, 4) * 2 + zh

    cp_in = pltpu.make_async_copy(pin, pinb, psem.at[0])
    cp_out = pltpu.make_async_copy(pout, poutb, psem.at[1])
    cp_out.start()
    cp_in.start()

    def load(k):
        p = lax.rem(y + 1 + k, 4)
        rows = pl.ds(pl.multiple_of(p * PART, PART), PART)
        return (
            pltpu.make_async_copy(og.at[rows], gbuf.at[p], gsem.at[k]),
            pltpu.make_async_copy(hid.at[rows], hbuf.at[p], hsem.at[k]),
        )

    for k in range(4):
        for cp in load(k):
            cp.start()

    barrier = pltpu.get_barrier_semaphore()

    def greet(k, c):
        pl.semaphore_signal(barrier, inc=1, device_id={"dp": lax.rem(dp + k, 32)}, device_id_type=MESH)
        return c

    lax.fori_loop(1, 32, greet, 0)
    for k in range(1, 4):
        pl.semaphore_signal(barrier, inc=1, device_id={"tensor": at_y(k)}, device_id_type=MESH)
    pl.semaphore_signal(barrier, inc=1, device_id={"tensor": y * 2 + 1 - zh}, device_id_type=MESH)

    hot = (own[...] - 8 * y == lax.broadcasted_iota(jnp.int32, (8, TOK), 0)).astype(F32)
    tri = (
        lax.broadcasted_iota(jnp.int32, (128, 128), 0) <= lax.broadcasted_iota(jnp.int32, (128, 128), 1)
    ).astype(BF)
    first = (lax.broadcasted_iota(jnp.int32, (8, 128), 0) * 128).astype(F32)
    carry = jnp.zeros((8, 1), F32)
    keys = []
    for b in range(8):
        h = hot[:, 128 * b : 128 * (b + 1)]
        rank = jnp.dot(h.astype(BF), tri, preferred_element_type=F32) + carry
        carry = carry + jnp.sum(h, 1, keepdims=True)
        keys.append(jnp.sum(h * (first + rank), 0, keepdims=True))
    key = jnp.concatenate(keys, 1).astype(jnp.int32) - 1
    idrow = jnp.broadcast_to((exi[...] + 1).astype(F32), (16, TOK)).astype(BF)
    for b in range(8):
        hit = key == lax.broadcasted_iota(jnp.int32, (128, TOK), 0) + 128 * b
        slots[128 * b : 128 * (b + 1), :] = hit.astype(F32).astype(BF)
        ids_send[b] = nt(idrow, slots[128 * b : 128 * (b + 1), :])[0:1, :]
    outer[COLS : COLS + 16, :] = jnp.ones((16, 128 * GROUP), BF)

    pl.semaphore_wait(barrier, 35)

    def ids_copy(k):
        dest = lax.rem(dp + k, 32)
        return remote(
            ids_send.at[lax.rem(dest, 8)], ids_recv.at[dp], i_ss.at[k], i_rs.at[dp], dp=dest
        )

    def ids_start(k, c):
        ids_copy(k).start()
        return c

    lax.fori_loop(1, 32, ids_start, 0)
    ids_recv[dp] = ids_send[lax.rem(dp, 8)]

    def rs_copy(k):
        p = lax.rem(y + 1 + k, 4)
        return remote(rs_send.at[k], rs_recv.at[y], rs_ss.at[k], rs_rs.at[y], tensor=p * 2 + zh)

    cp_out.wait()
    cp_in.wait()
    for k in range(4):
        p = lax.rem(y + 1 + k, 4)
        for cp in load(k):
            cp.wait()
        gp = nt(gbuf[p], poutb[...])
        xp = nt(hbuf[p], pinb[...])
        both = jnp.concatenate([xp, gp], 1).T
        if k < 3:
            rs_send[k] = both.astype(BF)
            rs_copy(k).start()
        else:
            part_own[...] = both

    total = part_own[...]
    for k in range(1, 4):
        src = lax.rem(y + k, 4)
        remote(
            rs_send.at[0], rs_recv.at[src], rs_ss.at[0], rs_rs.at[src], tensor=src * 2 + zh
        ).wait_recv()
        total = total + rs_recv[src].astype(F32)
    z_send[...] = total.astype(BF)
    z_copy = remote(z_send, z_recv, z_sem.at[0], z_sem.at[1], tensor=y * 2 + 1 - zh)
    z_copy.start()
    part_own[...] = total
    z_copy.wait_recv()
    vals[y] = (part_own[...] + z_recv[...].astype(F32)).astype(BF)

    def v_copy(k):
        return remote(vals.at[y], vals.at[y], v_ss.at[k], v_rs.at[y], tensor=at_y(k))

    for k in range(1, 4):
        v_copy(k).start()
    for k in range(1, 4):
        src = lax.rem(y + k, 4)
        remote(vals.at[src], vals.at[src], v_ss.at[k], v_rs.at[src], tensor=at_y(k)).wait_recv()

    for b in range(2):
        rows = slice(512 * b, 512 * (b + 1))
        routed = jnp.zeros((128, 512), F32)
        for p in range(4):
            routed = routed + nt(vals[p], slots[rows, PART * p : PART * (p + 1)])
        routed = routed.astype(BF)
        for o in range(4):
            piece = routed[:, 128 * o : 128 * (o + 1)]
            for s in range(4):
                sbuf[4 * b + o, s, 0:HALF, :] = piece[HALF * (s // 2) : HALF * (s // 2 + 1), :]
                sbuf[4 * b + o, s, HALF:R, :] = piece[R + HALF * (s % 2) : R + HALF * (s % 2 + 1), :]

    def tok_copy(k):
        dest = lax.rem(dp + k, 32)
        return remote(
            sbuf.at[lax.rem(dest, 8), dest // 8], rbuf.at[dp], t_ss.at[k], t_rs.at[dp], dp=dest
        )

    def tok_start(k, c):
        tok_copy(k).start()
        return c

    lax.fori_loop(1, 32, tok_start, 0)
    rbuf[dp] = sbuf[lax.rem(dp, 8), zl]
    acc[...] = jnp.zeros_like(acc)

    def kron(g, c):
        for s in range(GROUP):
            k = g * GROUP + s
            src = lax.rem(dp + 32 - k, 32)

            def arrived():
                remote(
                    ids_send.at[0], ids_recv.at[src], i_ss.at[0], i_rs.at[src], dp=src
                ).wait_recv()
                remote(
                    sbuf.at[0, 0], rbuf.at[src], t_ss.at[0], t_rs.at[src], dp=src
                ).wait_recv()

            if s == 0:
                pl.when(g > 0)(arrived)
            else:
                arrived()
            xr = rbuf[src, 0:HALF, :].astype(F32)
            gr = rbuf[src, HALF:R, :].astype(F32)
            lanes = slice(128 * s, 128 * (s + 1))
            for i in range(HALF):
                outer[HALF * i : HALF * (i + 1), lanes] = (xr[i : i + 1, :] * gr).astype(BF)
            ids = ids_recv[src].astype(jnp.int32)
            member[:, lanes] = (
                (ids == lax.broadcasted_iota(jnp.int32, (EX, 128), 0) + 1).astype(F32).astype(BF)
            )
        acc[...] += nt(outer[...], member[...])
        return c

    lax.fori_loop(0, 32 // GROUP, kron, 0)

    scale = 1.0 / jnp.maximum(acc[COLS : COLS + 1, :], 1.0)
    for b in range(COLS // 128):
        rows = slice(128 * b, 128 * (b + 1))
        bbuf[y, :, rows] = (acc[rows, :] * scale).T.astype(BF)

    yp, ym = at_y(1), at_y(3)
    low, high = pl.ds(0, 64), pl.ds(64, 64)
    before, after, across = lax.rem(y + 3, 4), lax.rem(y + 1, 4), lax.rem(y + 2, 4)
    r = lax.rem(x + 4 - 2 * zh, 4)
    mine = jnp.where(r < 2, r, 3 - r)
    other = 1 - mine

    def at_x(k):
        return zl * 8 + lax.rem(x + k, 4) * 2 + core

    b_up = remote(bbuf.at[y], bbuf.at[y], b_ss.at[0], b_rs.at[0], tensor=yp)
    b_down = remote(bbuf.at[y], bbuf.at[y], b_ss.at[1], b_rs.at[1], tensor=ym)
    b_up.start()
    b_down.start()

    def a_first(h, side):
        rows = pl.ds(64 * h, 64)
        return remote(
            bbuf.at[y, rows], abuf.at[mine * 2 + core, rows], a_ss.at[side, h], a_rs.at[mine, h],
            dp=at_x(1 if side == 0 else 3),
        )

    def a_next(h):
        rows = pl.ds(64 * h, 64)
        slot = abuf.at[mine * 2 + core, rows]
        return remote(
            slot, slot, a_ss.at[0, h], a_rs.at[mine, h], dp=at_x(1 + 2 * (r - 2))
        )

    def a_wait(which, h):
        slot = abuf.at[which * 2 + core, pl.ds(64 * h, 64)]
        remote(slot, slot, a_ss.at[0, h], a_rs.at[which, h], dp=at_x(1)).wait_recv()

    @pl.when(r < 2)
    def _():
        for h in range(2):
            a_first(h, 0).start()
            a_first(h, 1).start()
        abuf[mine * 2 + core] = bbuf[y]

    @pl.when(r >= 2)
    def _():
        for h in range(2):
            a_wait(mine, h)
            a_next(h).start()

    twin = dp + 1 - 2 * core

    def x_copy(which):
        slot = abuf.at[which * 2 + core]
        return remote(slot, slot, x_ss.at[which], x_rs.at[which], dp=twin)

    x_copy(mine).start()

    remote(bbuf.at[before], bbuf.at[before], b_ss.at[0], b_rs.at[0], tensor=ym).wait_recv()
    b_fwd_up = remote(bbuf.at[before, low], bbuf.at[before, low], b_ss.at[2], b_rs.at[2], tensor=yp)
    b_fwd_up.start()
    remote(bbuf.at[after], bbuf.at[after], b_ss.at[1], b_rs.at[1], tensor=yp).wait_recv()
    b_fwd_down = remote(bbuf.at[after, high], bbuf.at[after, high], b_ss.at[3], b_rs.at[3], tensor=ym)
    b_fwd_down.start()

    for h in range(2):
        a_wait(other, h)
    x_copy(other).start()
    for which in range(2):
        slot = abuf.at[which * 2 + 1 - core]
        remote(slot, slot, x_ss.at[which], x_rs.at[which], dp=twin).wait_recv()

    rows_a = abuf[...].reshape(4 * EX, COLS)

    def c_copy(q):
        return remote(c_send.at[q], c_recv.at[zl], c_ss.at[q], c_rs.at[zl], dp=q * 8 + x * 2 + core)

    for k in (0, 1, 3, 2):
        q = lax.rem(y + k, 4)
        if k == 2:
            remote(
                bbuf.at[across, low], bbuf.at[across, low], b_ss.at[2], b_rs.at[2], tensor=ym
            ).wait_recv()
            remote(
                bbuf.at[across, high], bbuf.at[across, high], b_ss.at[3], b_rs.at[3], tensor=yp
            ).wait_recv()
        block = nt(rows_a, bbuf[q]) * (1.0 / R)

        @pl.when(q == zl)
        def _():
            keep[...] = block

        @pl.when(q != zl)
        def _():
            c_send[q] = block.astype(BF)
            c_copy(q).start()

    result = keep[...]
    for k in range(1, 4):
        src = lax.rem(zl + k, 4)
        remote(c_send.at[src], c_recv.at[src], c_ss.at[src], c_rs.at[src], dp=src * 8 + x * 2 + core).wait_recv()
        result = result + c_recv[src].astype(F32)
    out[...] = result

    def left(k, c):
        ids_copy(k).wait_send()
        tok_copy(k).wait_send()
        return c

    lax.fori_loop(1, 32, left, 0)
    for k in range(3):
        rs_copy(k).wait_send()
        v_copy(k + 1).wait_send()
        c_copy(lax.rem(zl + k + 1, 4)).wait_send()
    z_copy.wait_send()
    for cp in (b_up, b_down, b_fwd_up, b_fwd_down, x_copy(0), x_copy(1)):
        cp.wait_send()

    @pl.when(r < 2)
    def _():
        for h in range(2):
            a_first(h, 0).wait_send()
            a_first(h, 1).wait_send()

    @pl.when(r >= 2)
    def _():
        for h in range(2):
            a_next(h).wait_send()


def body(hidden, out_grad, proj_in, proj_out, owner_ids, example_ids):
    wide, model = hidden.shape[1], out_grad.shape[1]
    hbm = pl.BlockSpec(memory_space=pltpu.HBM)
    vmem = pl.BlockSpec(memory_space=pltpu.VMEM)
    dma = pltpu.SemaphoreType.DMA
    return pl.pallas_call(
        kernel,
        out_shape=jax.ShapeDtypeStruct((4 * EX, EX), F32),
        in_specs=[hbm, hbm, hbm, hbm, vmem, vmem],
        out_specs=vmem,
        scratch_shapes=[
            pltpu.VMEM((4, PART, wide), BF),
            pltpu.VMEM((4, PART, model), BF),
            pltpu.VMEM((R, wide), BF),
            pltpu.VMEM((R, model), BF),
            pltpu.VMEM((2 * R, PART), F32),
            pltpu.VMEM((3, 2 * R, PART), BF),
            pltpu.VMEM((4, 2 * R, PART), BF),
            pltpu.VMEM((2 * R, PART), BF),
            pltpu.VMEM((2 * R, PART), BF),
            pltpu.VMEM((4, 2 * R, PART), BF),
            pltpu.VMEM((8 * 128, TOK), BF),
            pltpu.VMEM((8, 1, 128), F32),
            pltpu.VMEM((32, 1, 128), F32),
            pltpu.VMEM((8, 4, R, 128), BF),
            pltpu.VMEM((32, R, 128), BF),
            pltpu.VMEM((COLS + 16, 128 * GROUP), BF),
            pltpu.VMEM((EX, 128 * GROUP), BF),
            pltpu.VMEM((COLS + 16, EX), F32),
            pltpu.VMEM((4, EX, COLS), BF),
            pltpu.VMEM((4, EX, COLS), BF),
            pltpu.VMEM((4 * EX, EX), F32),
            pltpu.VMEM((4, 4 * EX, EX), BF),
            pltpu.VMEM((4, 4 * EX, EX), BF),
            dma((4,)), dma((4,)), dma((2,)), dma((3,)), dma((4,)), dma((2,)), dma((4,)), dma((4,)),
            dma((32,)), dma((32,)), dma((32,)), dma((32,)),
            dma((2, 2)), dma((2, 2)), dma((2,)), dma((2,)), dma((4,)), dma((4,)), dma((4,)), dma((4,)),
        ],
        compiler_params=pltpu.CompilerParams(
            collective_id=0, has_side_effects=True, vmem_limit_bytes=48 * 1024 * 1024
        ),
        name="per_example_kernel",
    )(hidden, out_grad, proj_in.T, proj_out.T, owner_ids.reshape(1, TOK), example_ids.reshape(1, TOK))


def solution(mesh):
    in_specs = (
        P("dp", "tensor"),
        P("dp", "tensor"),
        P("tensor", None),
        P("tensor", None),
        P("dp", None),
        P("dp"),
    )
    out_specs = P("tensor", "dp")
    return jax.shard_map(body, mesh=mesh, in_specs=in_specs, out_specs=out_specs, check_vma=False)
```

time: 377 us -> 76.5 us (0.20)
  waiting for transfers between devices: 286 us -> 0 us
  Pallas kernels: 0 us -> 70.4 us
  starting transfers between devices: 18.9 us -> 0 us
  matrix products: 17.1 us -> 0 us
  local copies, waits for them, and re-layouts: 22.3 us -> 5.59 us
  other arithmetic: 16.1 us -> 0 us
  between operations: 13.3 us -> 0.01 us
    reduce_scatter x1 -> x0, waiting for transfers between devices: 91.9 us -> none  [body(): return lax.psum_scatter(products, 'tensor', scatter_dimension=0, tiled=True)]
    psum x1 -> x0, waiting for transfers between devices: 85.1 us -> none  [body(): send_rows = lax.psum(jnp.concatenate([x_part, g_part], 1), 'tensor')]
    pallas_call x0 -> x1, Pallas kernels: none -> 70.4 us  [body(): pl.pallas_call(kernel, out_shape=jax.ShapeDtypeStruct((4 * EX, EX), F32),...]
    all_gather x1 -> x0, waiting for transfers between devices: 61.2 us -> none  [body(): lax.all_gather(grads, 'dp', axis=0, tiled=True)]
    all_to_all x2 -> x0, waiting for transfers between devices: 47.6 us -> none  [the longest x1 47.6 us: body(): lax.all_to_all(row_buffer.reshape(groups, capacity, columns), 'dp', split...]
    all_to_all x2 -> x0, starting transfers between devices: 18.8 us -> none  [the longest x1 9.49 us: body(): lax.all_to_all(row_buffer.reshape(groups, capacity, columns), 'dp', split...]
    dot_general x5 -> x0, matrix products: 17.1 us -> none  [the longest x1 5.56 us: body(): x_part = jnp.dot(hidden, proj_in, preferred_element_type=jnp.float32)]
    scatter x2 -> x0, local copies, waits for them, and re-layouts: 9.35 us -> none  [the longest x1 4.89 us: body(): id_buffer = jnp.full((groups * capacity,), -1.0, jnp.float32).at[target]....]
  transfers between devices with their start and end apart: 5 -> 0, of which waited for: 4 -> 0; matrix products, arithmetic and copies ran while one was open for 5% -> 0% of each run, Pallas kernels for 0% -> 0%
where the time goes in v1:
time: 76.5 us; the launch traced here: 76 us
  Pallas kernels  70.4 us (92%)
  local copies, waits for them, and re-layouts  5.59 us (7%)
    pallas_call x1, Pallas kernels, body(): pl.pallas_call(kernel, out_shape=jax.ShapeDtypeStruct((4 * EX, EX), F32),...  70.4 us
    unnamed x11, local copies, waits for them, and re-layouts  5.59 us

profile of v1, /device:TPU:21, one launch (start us, length us, event | category | flops | bytes accessed | tf_op | source)
XLA Modules:
  0.0 76.0 jit_solution(3139068493444251546)
XLA Ops:
  0.0 0.0 copy-start
  0.0 1.6 %copy-done = bf16[1024,1024]{1,0:T(8,128)(2,1)S(1)} copy-done((bf16[1024,1024]{1,0:T(8,128)(2,1)S(1)}, bf16[1024,1024]{1,0:T(8,128)(2,1)}, u32[]{:S(2)}) %copy-start) | copy-done | bytes 2097176
  1.6 0.0 copy-start.1
  1.6 1.0 %copy-done.1 = bf16[3584,64]{0,1:T(8,128)(2,1)S(1)} copy-done((bf16[3584,64]{0,1:T(8,128)(2,1)S(1)}, bf16[3584,64]{0,1:T(8,128)(2,1)}, u32[]{:S(2)}) %copy-start.1) | copy-done | bytes 458776
  2.6 0.0 copy-start.2
  2.6 0.9 %copy-done.2 = bf16[1024,64]{0,1:T(8,128)(2,1)S(1)} copy-done((bf16[1024,64]{0,1:T(8,128)(2,1)S(1)}, bf16[1024,64]{0,1:T(8,128)(2,1)}, u32[]{:S(2)}) %copy-start.2) | copy-done | bytes 131096
  3.5 0.0 copy-start.3
  3.5 0.7 copy-done.3
  4.2 0.0 copy-start.4
  4.2 0.7 copy-done.4
  4.9 70.4 %per_example_kernel.1 = f32[512,128]{1,0:T(8,128)S(1)} custom-call(bf16[1024,3584]{1,0:T(8,128)(2,1)} %hid.1, bf16[1024,1024]{1,0:T(8,128)(2,1)S(1)} %copy-done, bf16[64,3584]{1,0:T(8,128)(2,1)S(1)} %bitcast.4, bf16[64,1024]{1,0:T(8,128)(2,1)S(1)} %bitcast.5, s32[1,1024]{1,0:T(1,128)S(1)} %bitcast.6, s32[1,1024]{1,0:T(1,128)S(1)} %bitcast.7), custom_call_target="tpu_custom_call" | custom-call | tf_op jit(solution)/shard_map/per_example_kernel/pallas_call | solution.py:347
  75.3 0.7 copy.8
Async XLA Ops:
  0.0 1.6 %copy-start = (bf16[1024,1024]{1,0:T(8,128)(2,1)S(1)}, bf16[1024,1024]{1,0:T(8,128)(2,1)}, u32[]{:S(2)}) copy-start(bf16[1024,1024]{1,0:T(8,128)(2,1)} %og.1) | copy-start | bytes 6291460
  1.6 1.0 %copy-start.1 = (bf16[3584,64]{0,1:T(8,128)(2,1)S(1)}, bf16[3584,64]{0,1:T(8,128)(2,1)}, u32[]{:S(2)}) copy-start(bf16[3584,64]{0,1:T(8,128)(2,1)} %param.8) | copy-start | bytes 1376260
  2.6 0.9 %copy-start.2 = (bf16[1024,64]{0,1:T(8,128)(2,1)S(1)}, bf16[1024,64]{0,1:T(8,128)(2,1)}, u32[]{:S(2)}) copy-start(bf16[1024,64]{0,1:T(8,128)(2,1)} %param.9) | copy-start | bytes 393220
  3.5 0.7 copy-start.3
  4.2 0.7 copy-start.4

commit v2 on v1

v2 whole, which is shorter than its diff:
```python
import jax
import jax.numpy as jnp
from jax import lax
from jax.experimental import pallas as pl
from jax.experimental.pallas import tpu as pltpu
from jax.sharding import PartitionSpec as P

TOK = 1024
PART = 256
EX = 128
R = 64
HALF = 32
COLS = HALF * HALF
GROUP = 4
NT = (((1,), (1,)), ((), ()))
MESH = pl.DeviceIdType.MESH
BF = jnp.bfloat16
F32 = jnp.float32


def nt(a, b):
    return lax.dot_general(a, b, NT, preferred_element_type=F32)


def kernel(
    hid, og, pin, pout, own_in, exi_in, out,
    own, exi,
    hbuf, gbuf, pinb, poutb, part_own, rs_send, rs_recv, z_send, z_recv, vals, slots,
    routed, sbuf, rbuf, outer, member, acc, bbuf, abuf, keep, c_send, c_recv,
    hsem, gsem, psem, rs_ss, rs_rs, z_ss, z_rs, v_ss, v_rs, t_ss, t_rs,
    a_ss, a_rs, x_ss, x_rs, b_ss, b_rs, c_ss, c_rs,
):
    dp = lax.axis_index("dp")
    tn = lax.axis_index("tensor")
    y = tn // 2
    zh = lax.rem(tn, 2)
    zl = dp // 8
    x = lax.rem(dp // 2, 4)
    core = lax.rem(dp, 2)

    def remote(src, dst, ss, rs, **where):
        return pltpu.make_async_remote_copy(
            src_ref=src, dst_ref=dst, send_sem=ss, recv_sem=rs,
            device_id=where, device_id_type=MESH,
        )

    def at_y(k):
        return lax.rem(y + k, 4) * 2 + zh

    cp_in = pltpu.make_async_copy(pin, pinb, psem.at[0])
    cp_out = pltpu.make_async_copy(pout, poutb, psem.at[1])
    cp_own = pltpu.make_async_copy(own_in, own, psem.at[2])
    cp_exi = pltpu.make_async_copy(exi_in, exi, psem.at[3])
    cp_own.start()
    cp_exi.start()
    cp_out.start()
    cp_in.start()

    def load(k):
        p = lax.rem(y + 1 + k, 4)
        rows = pl.ds(pl.multiple_of(p * PART, PART), PART)
        return (
            pltpu.make_async_copy(og.at[rows], gbuf.at[p], gsem.at[k]),
            pltpu.make_async_copy(hid.at[rows], hbuf.at[p], hsem.at[k]),
        )

    for k in range(4):
        for cp in load(k):
            cp.start()

    barrier = pltpu.get_barrier_semaphore()

    def greet(k, c):
        pl.semaphore_signal(barrier, inc=1, device_id={"dp": lax.rem(dp + k, 32)}, device_id_type=MESH)
        return c

    lax.fori_loop(1, 32, greet, 0)
    for k in range(1, 4):
        pl.semaphore_signal(barrier, inc=1, device_id={"tensor": at_y(k)}, device_id_type=MESH)
    pl.semaphore_signal(barrier, inc=1, device_id={"tensor": y * 2 + 1 - zh}, device_id_type=MESH)

    cp_own.wait()
    cp_exi.wait()
    hot = (own[...] - 8 * y == lax.broadcasted_iota(jnp.int32, (8, TOK), 0)).astype(F32)
    tri = (
        lax.broadcasted_iota(jnp.int32, (128, 128), 0) <= lax.broadcasted_iota(jnp.int32, (128, 128), 1)
    ).astype(BF)
    first = (lax.broadcasted_iota(jnp.int32, (8, 128), 0) * 128).astype(F32)
    carry = jnp.zeros((8, 1), F32)
    keys = []
    for b in range(8):
        h = hot[:, 128 * b : 128 * (b + 1)]
        rank = jnp.dot(h.astype(BF), tri, preferred_element_type=F32) + carry
        carry = carry + jnp.sum(h, 1, keepdims=True)
        keys.append(jnp.sum(h * (first + rank), 0, keepdims=True))
    order = [2 * p + ch for ch in range(2) for p in range(4)]
    key = jnp.concatenate([keys[b] for b in order], 1).astype(jnp.int32) - 1
    idrow = (exi[...] + 1).astype(F32)
    idrow = jnp.concatenate([idrow[:, 128 * b : 128 * (b + 1)] for b in order], 1)
    idrow = jnp.broadcast_to(idrow, (16, TOK)).astype(BF)
    for o in range(8):
        hit = key == lax.broadcasted_iota(jnp.int32, (128, TOK), 0) + 128 * o
        slots[128 * o : 128 * (o + 1), :] = hit.astype(F32).astype(BF)
        ids = nt(idrow, slots[128 * o : 128 * (o + 1), :])[0:8, :].astype(BF)
        for q in range(4):
            sbuf[o, q, R : R + 8, :] = ids
    outer[COLS : COLS + 16, :] = jnp.ones((16, 128 * GROUP), BF)
    acc[...] = jnp.zeros_like(acc)

    def rs_copy(k):
        p = lax.rem(y + 1 + k, 4)
        return remote(rs_send.at[k], rs_recv.at[y], rs_ss.at[k], rs_rs.at[y], tensor=p * 2 + zh)

    def project(k):
        p = lax.rem(y + 1 + k, 4)
        for cp in load(k):
            cp.wait()
        gp = nt(gbuf[p], poutb[...])
        xp = nt(hbuf[p], pinb[...])
        return jnp.concatenate([xp, gp], 1).T

    cp_out.wait()
    cp_in.wait()
    for k in range(3):
        both = project(k).astype(BF)
        rs_send[k, 0] = both[:, :128]
        rs_send[k, 1] = both[:, 128:]
    pl.semaphore_wait(barrier, 35)
    for k in range(3):
        rs_copy(k).start()
    both = project(3)
    part_own[0] = both[:, :128]
    part_own[1] = both[:, 128:]

    for k in range(1, 4):
        src = lax.rem(y + k, 4)
        remote(
            rs_send.at[0], rs_recv.at[src], rs_ss.at[0], rs_rs.at[src], tensor=src * 2 + zh
        ).wait_recv()

    def z_copy(ch):
        return remote(z_send.at[ch], z_recv.at[ch], z_ss.at[ch], z_rs.at[ch], tensor=y * 2 + 1 - zh)

    for ch in range(2):
        total = part_own[ch]
        for k in range(1, 4):
            total = total + rs_recv[lax.rem(y + k, 4), ch].astype(F32)
        z_send[ch] = total.astype(BF)
        z_copy(ch).start()
        part_own[ch] = total

    def v_copy(ch, k):
        return remote(vals.at[ch, y], vals.at[ch, y], v_ss.at[ch, k], v_rs.at[ch, y], tensor=at_y(k))

    for ch in range(2):
        z_copy(ch).wait_recv()
        vals[ch, y] = (part_own[ch] + z_recv[ch].astype(F32)).astype(BF)
        for k in range(1, 4):
            v_copy(ch, k).start()

    for ch in range(2):
        for k in range(1, 4):
            src = lax.rem(y + k, 4)
            remote(
                vals.at[ch, src], vals.at[ch, src], v_ss.at[ch, k], v_rs.at[ch, src], tensor=at_y(k)
            ).wait_recv()
        part = jnp.concatenate([vals[ch, p] for p in range(4)], 1)
        for b in range(2):
            rows = slice(512 * b, 512 * (b + 1))
            placed = nt(part, slots[rows, 512 * ch : 512 * (ch + 1)])
            if ch == 0:
                routed[:, rows] = placed
                continue
            placed = (placed + routed[:, rows]).astype(BF)
            for o in range(4):
                piece = placed[:, 128 * o : 128 * (o + 1)]
                for q in range(4):
                    sbuf[4 * b + o, q, 0:HALF, :] = piece[HALF * (q // 2) : HALF * (q // 2 + 1), :]
                    sbuf[4 * b + o, q, HALF:R, :] = piece[R + HALF * (q % 2) : R + HALF * (q % 2 + 1), :]

    def tok_copy(k):
        dest = lax.rem(dp + k, 32)
        return remote(
            sbuf.at[lax.rem(dest, 8), dest // 8], rbuf.at[dp], t_ss.at[k], t_rs.at[dp], dp=dest
        )

    def tok_start(k, c):
        tok_copy(k).start()
        return c

    lax.fori_loop(1, 32, tok_start, 0)
    rbuf[dp] = sbuf[lax.rem(dp, 8), zl]

    def kron(g, c):
        for s in range(GROUP):
            k = g * GROUP + s
            src = lax.rem(dp + 32 - k, 32)

            def arrived():
                remote(
                    sbuf.at[0, 0], rbuf.at[src], t_ss.at[0], t_rs.at[src], dp=src
                ).wait_recv()

            if s == 0:
                pl.when(g > 0)(arrived)
            else:
                arrived()
            xr = rbuf[src, 0:HALF, :].astype(F32)
            gr = rbuf[src, HALF:R, :].astype(F32)
            lanes = slice(128 * s, 128 * (s + 1))
            for i in range(HALF):
                outer[HALF * i : HALF * (i + 1), lanes] = (xr[i : i + 1, :] * gr).astype(BF)
            ids = rbuf[src, R : R + 8, :].astype(F32)[0:1, :].astype(jnp.int32)
            member[:, lanes] = (
                (ids == lax.broadcasted_iota(jnp.int32, (EX, 128), 0) + 1).astype(F32).astype(BF)
            )
        acc[...] += nt(outer[...], member[...])
        return c

    lax.fori_loop(0, 32 // GROUP, kron, 0)

    scale = 1.0 / jnp.maximum(acc[COLS : COLS + 1, :], 1.0)
    for b in range(COLS // 128):
        rows = slice(128 * b, 128 * (b + 1))
        bbuf[y, :, rows] = (acc[rows, :] * scale).T.astype(BF)

    yp, ym = at_y(1), at_y(3)
    low, high = pl.ds(0, 64), pl.ds(64, 64)
    before, after, across = lax.rem(y + 3, 4), lax.rem(y + 1, 4), lax.rem(y + 2, 4)
    r = lax.rem(x + 4 - 2 * zh, 4)
    mine = jnp.where(r < 2, r, 3 - r)
    other = 1 - mine

    def at_x(k):
        return zl * 8 + lax.rem(x + k, 4) * 2 + core

    b_up = remote(bbuf.at[y], bbuf.at[y], b_ss.at[0], b_rs.at[0], tensor=yp)
    b_down = remote(bbuf.at[y], bbuf.at[y], b_ss.at[1], b_rs.at[1], tensor=ym)
    b_up.start()
    b_down.start()

    def a_first(h, side):
        rows = pl.ds(64 * h, 64)
        return remote(
            bbuf.at[y, rows], abuf.at[mine * 2 + core, rows], a_ss.at[side, h], a_rs.at[mine, h],
            dp=at_x(1 if side == 0 else 3),
        )

    def a_next(h):
        rows = pl.ds(64 * h, 64)
        slot = abuf.at[mine * 2 + core, rows]
        return remote(
            slot, slot, a_ss.at[0, h], a_rs.at[mine, h], dp=at_x(1 + 2 * (r - 2))
        )

    def a_wait(which, h):
        slot = abuf.at[which * 2 + core, pl.ds(64 * h, 64)]
        remote(slot, slot, a_ss.at[0, h], a_rs.at[which, h], dp=at_x(1)).wait_recv()

    @pl.when(r < 2)
    def _():
        for h in range(2):
            a_first(h, 0).start()
            a_first(h, 1).start()
        abuf[mine * 2 + core] = bbuf[y]

    @pl.when(r >= 2)
    def _():
        for h in range(2):
            a_wait(mine, h)
            a_next(h).start()

    twin = dp + 1 - 2 * core

    def x_copy(which):
        slot = abuf.at[which * 2 + core]
        return remote(slot, slot, x_ss.at[which], x_rs.at[which], dp=twin)

    def x_wait(which):
        slot = abuf.at[which * 2 + 1 - core]
        remote(slot, slot, x_ss.at[which], x_rs.at[which], dp=twin).wait_recv()

    def c_copy(q, which):
        rows = pl.ds(pl.multiple_of(2 * EX * which, 2 * EX), 2 * EX)
        return remote(
            c_send.at[q, rows], c_recv.at[zl, rows], c_ss.at[q, which], c_rs.at[zl, which],
            dp=q * 8 + x * 2 + core,
        )

    def block(which, q):
        rows = pl.ds(pl.multiple_of(2 * EX * which, 2 * EX), 2 * EX)
        a = abuf[pl.ds(which * 2, 2)].reshape(2 * EX, COLS)
        product = nt(a, bbuf[q]) * (1.0 / R)

        @pl.when(q == zl)
        def _():
            keep[rows, :] = product

        @pl.when(q != zl)
        def _():
            c_send[q, rows, :] = product.astype(BF)
            c_copy(q, which).start()

    x_copy(mine).start()
    x_wait(mine)
    block(mine, y)
    remote(bbuf.at[before], bbuf.at[before], b_ss.at[0], b_rs.at[0], tensor=ym).wait_recv()
    b_fwd_up = remote(bbuf.at[before, low], bbuf.at[before, low], b_ss.at[2], b_rs.at[2], tensor=yp)
    b_fwd_up.start()
    remote(bbuf.at[after], bbuf.at[after], b_ss.at[1], b_rs.at[1], tensor=yp).wait_recv()
    b_fwd_down = remote(bbuf.at[after, high], bbuf.at[after, high], b_ss.at[3], b_rs.at[3], tensor=ym)
    b_fwd_down.start()
    block(mine, after)
    block(mine, before)
    for h in range(2):
        a_wait(other, h)
    x_copy(other).start()
    x_wait(other)
    block(other, y)
    block(other, after)
    block(other, before)
    remote(bbuf.at[across, low], bbuf.at[across, low], b_ss.at[2], b_rs.at[2], tensor=ym).wait_recv()
    remote(bbuf.at[across, high], bbuf.at[across, high], b_ss.at[3], b_rs.at[3], tensor=yp).wait_recv()
    block(mine, across)
    block(other, across)

    result = keep[...]
    for k in range(1, 4):
        src = lax.rem(zl + k, 4)
        for which in range(2):
            rows = slice(2 * EX * which, 2 * EX * (which + 1))
            remote(
                c_send.at[src, rows], c_recv.at[src, rows], c_ss.at[src, which], c_rs.at[src, which],
                dp=src * 8 + x * 2 + core,
            ).wait_recv()
        result = result + c_recv[src].astype(F32)
    out[...] = result

    def left(k, c):
        tok_copy(k).wait_send()
        return c

    lax.fori_loop(1, 32, left, 0)
    for k in range(3):
        rs_copy(k).wait_send()
        for h in range(2):
            v_copy(h, k + 1).wait_send()
            c_copy(lax.rem(zl + k + 1, 4), h).wait_send()
    for h in range(2):
        z_copy(h).wait_send()
    for cp in (b_up, b_down, b_fwd_up, b_fwd_down, x_copy(0), x_copy(1)):
        cp.wait_send()

    @pl.when(r < 2)
    def _():
        for h in range(2):
            a_first(h, 0).wait_send()
            a_first(h, 1).wait_send()

    @pl.when(r >= 2)
    def _():
        for h in range(2):
            a_next(h).wait_send()


def body(hidden, out_grad, proj_in, proj_out, owner_ids, example_ids):
    wide, model = hidden.shape[1], out_grad.shape[1]
    hbm = pl.BlockSpec(memory_space=pltpu.HBM)
    vmem = pl.BlockSpec(memory_space=pltpu.VMEM)
    dma = pltpu.SemaphoreType.DMA
    return pl.pallas_call(
        kernel,
        out_shape=jax.ShapeDtypeStruct((4 * EX, EX), F32),
        in_specs=[hbm] * 6,
        out_specs=vmem,
        scratch_shapes=[
            pltpu.VMEM((1, TOK), jnp.int32),
            pltpu.VMEM((1, TOK), jnp.int32),
            pltpu.VMEM((4, PART, wide), BF),
            pltpu.VMEM((4, PART, model), BF),
            pltpu.VMEM((R, wide), BF),
            pltpu.VMEM((R, model), BF),
            pltpu.VMEM((2, 2 * R, 128), F32),
            pltpu.VMEM((3, 2, 2 * R, 128), BF),
            pltpu.VMEM((4, 2, 2 * R, 128), BF),
            pltpu.VMEM((2, 2 * R, 128), BF),
            pltpu.VMEM((2, 2 * R, 128), BF),
            pltpu.VMEM((2, 4, 2 * R, 128), BF),
            pltpu.VMEM((8 * 128, TOK), BF),
            pltpu.VMEM((2 * R, 8 * 128), F32),
            pltpu.VMEM((8, 4, R + 8, 128), BF),
            pltpu.VMEM((32, R + 8, 128), BF),
            pltpu.VMEM((COLS + 16, 128 * GROUP), BF),
            pltpu.VMEM((EX, 128 * GROUP), BF),
            pltpu.VMEM((COLS + 16, EX), F32),
            pltpu.VMEM((4, EX, COLS), BF),
            pltpu.VMEM((4, EX, COLS), BF),
            pltpu.VMEM((4 * EX, EX), F32),
            pltpu.VMEM((4, 4 * EX, EX), BF),
            pltpu.VMEM((4, 4 * EX, EX), BF),
            dma((4,)), dma((4,)), dma((4,)), dma((3,)), dma((4,)), dma((2,)), dma((2,)),
            dma((2, 4)), dma((2, 4)), dma((32,)), dma((32,)),
            dma((2, 2)), dma((2, 2)), dma((2,)), dma((2,)), dma((4,)), dma((4,)), dma((4, 2)), dma((4, 2)),
        ],
        compiler_params=pltpu.CompilerParams(
            collective_id=0, has_side_effects=True, vmem_limit_bytes=60 * 1024 * 1024
        ),
        name="per_example_kernel",
    )(hidden, out_grad, proj_in.T, proj_out.T, owner_ids.reshape(1, TOK), example_ids.reshape(1, TOK))


def solution(mesh):
    in_specs = (
        P("dp", "tensor"),
        P("dp", "tensor"),
        P("tensor", None),
        P("tensor", None),
        P("dp", None),
        P("dp"),
    )
    out_specs = P("tensor", "dp")
    return jax.shard_map(body, mesh=mesh, in_specs=in_specs, out_specs=out_specs, check_vma=False)
```

time: 76.5 us -> 70.3 us (0.919)
  local copies, waits for them, and re-layouts: 5.59 us -> 1.67 us
  Pallas kernels: 70.4 us -> 68.5 us
    unnamed x11 -> x1, local copies, waits for them, and re-layouts: 5.59 us -> 1.67 us
    pallas_call x1, Pallas kernels: 70.4 us -> 68.5 us  [body(): pl.pallas_call(kernel, out_shape=jax.ShapeDtypeStruct((4 * EX, EX), F32),...]
where the time goes in v2:
time: 70.3 us; the launch traced here: 70.2 us
  Pallas kernels  68.5 us (97%)
  local copies, waits for them, and re-layouts  1.67 us (2%)
    pallas_call x1, Pallas kernels, body(): pl.pallas_call(kernel, out_shape=jax.ShapeDtypeStruct((4 * EX, EX), F32),...  68.5 us
    unnamed x1, local copies, waits for them, and re-layouts  1.67 us

profile of v2, /device:TPU:21, one launch (start us, length us, event | category | flops | bytes accessed | tf_op | source)
XLA Modules:
  0.0 70.2 jit_solution(1842853951537956556)
XLA Ops:
  0.0 68.5 %per_example_kernel.1 = f32[512,128]{1,0:T(8,128)} custom-call(bf16[1024,3584]{1,0:T(8,128)(2,1)} %hid.1, bf16[1024,1024]{1,0:T(8,128)(2,1)} %og.1, bf16[64,3584]{1,0:T(8,128)(2,1)} %bitcast.4, bf16[64,1024]{1,0:T(8,128)(2,1)} %bitcast.5, s32[1,1024]{1,0:T(1,128)} %bitcast.6, s32[1,1024]{1,0:T(1,128)} %bitcast.7), custom_call_target="tpu_custom_call" | custom-call | tf_op jit(solution)/shard_map/per_example_kernel/pallas_call | solution.py:371
  68.5 1.7 %copy.8 = f32[512,128]{1,0:T(8,128)} copy(f32[512,128]{1,0:T(8,128)} %per_example_kernel.1) | data formatting | bytes 524288

commit v3 on v2

--- a/solution.py
+++ b/solution.py
@@ -12,6 +12,8 @@
 HALF = 32
 COLS = HALF * HALF
 GROUP = 4
+CHUNKS = 4
+WIDE = COLS // CHUNKS
 NT = (((1,), (1,)), ((), ()))
 MESH = pl.DeviceIdType.MESH
 BF = jnp.bfloat16
@@ -125,8 +127,8 @@
         both = project(k).astype(BF)
         rs_send[k, 0] = both[:, :128]
         rs_send[k, 1] = both[:, 128:]
-    pl.semaphore_wait(barrier, 35)
-    for k in range(3):
+        if k == 0:
+            pl.semaphore_wait(barrier, 35)
         rs_copy(k).start()
     both = project(3)
     part_own[0] = both[:, :128]
@@ -178,23 +180,31 @@
                     sbuf[4 * b + o, q, 0:HALF, :] = piece[HALF * (q // 2) : HALF * (q // 2 + 1), :]
                     sbuf[4 * b + o, q, HALF:R, :] = piece[R + HALF * (q % 2) : R + HALF * (q % 2 + 1), :]
 
-    def tok_copy(k):
-        dest = lax.rem(dp + k, 32)
+    xc = lax.rem(dp, 8)
+
+    def tok_copy(dz, j):
+        zq, xq = lax.rem(zl + dz, 4), lax.rem(xc + j, 8)
         return remote(
-            sbuf.at[lax.rem(dest, 8), dest // 8], rbuf.at[dp], t_ss.at[k], t_rs.at[dp], dp=dest
-        )
-
-    def tok_start(k, c):
-        tok_copy(k).start()
-        return c
-
-    lax.fori_loop(1, 32, tok_start, 0)
-    rbuf[dp] = sbuf[lax.rem(dp, 8), zl]
+            sbuf.at[xq, zq], rbuf.at[dp], t_ss.at[dz * 8 + j], t_rs.at[dp], dp=zq * 8 + xq
+        )
+
+    def tok_start(dz):
+        def step(j, c):
+            tok_copy(dz, j).start()
+            return c
+
+        lax.fori_loop(1 if dz == 0 else 0, 8, step, 0)
+
+    for dz in (2, 1, 3, 0):
+        tok_start(dz)
+    rbuf[dp] = sbuf[xc, zl]
 
     def kron(g, c):
+        half = g // 2
+        dz = jnp.where(half < 2, half, 5 - half)
         for s in range(GROUP):
-            k = g * GROUP + s
-            src = lax.rem(dp + 32 - k, 32)
+            j = lax.rem(g, 2) * GROUP + s
+            src = lax.rem(zl + 4 - dz, 4) * 8 + lax.rem(xc + 8 - j, 8)
 
             def arrived():
                 remote(
@@ -219,66 +229,61 @@
 
     lax.fori_loop(0, 32 // GROUP, kron, 0)
 
-    scale = 1.0 / jnp.maximum(acc[COLS : COLS + 1, :], 1.0)
-    for b in range(COLS // 128):
-        rows = slice(128 * b, 128 * (b + 1))
-        bbuf[y, :, rows] = (acc[rows, :] * scale).T.astype(BF)
-
     yp, ym = at_y(1), at_y(3)
-    low, high = pl.ds(0, 64), pl.ds(64, 64)
     before, after, across = lax.rem(y + 3, 4), lax.rem(y + 1, 4), lax.rem(y + 2, 4)
     r = lax.rem(x + 4 - 2 * zh, 4)
     mine = jnp.where(r < 2, r, 3 - r)
     other = 1 - mine
+    twin = dp + 1 - 2 * core
 
     def at_x(k):
         return zl * 8 + lax.rem(x + k, 4) * 2 + core
 
-    b_up = remote(bbuf.at[y], bbuf.at[y], b_ss.at[0], b_rs.at[0], tensor=yp)
-    b_down = remote(bbuf.at[y], bbuf.at[y], b_ss.at[1], b_rs.at[1], tensor=ym)
-    b_up.start()
-    b_down.start()
-
-    def a_first(h, side):
-        rows = pl.ds(64 * h, 64)
+    def b_copy(q, n, way):
         return remote(
-            bbuf.at[y, rows], abuf.at[mine * 2 + core, rows], a_ss.at[side, h], a_rs.at[mine, h],
+            bbuf.at[q, n], bbuf.at[q, n], b_ss.at[q, n, way], b_rs.at[q, n], tensor=yp if way == 0 else ym
+        )
+
+    def b_wait(q, n):
+        b_copy(q, n, 0).wait_recv()
+
+    def a_first(n, side):
+        return remote(
+            bbuf.at[y, n], abuf.at[mine * 2 + core, n], a_ss.at[side, n], a_rs.at[mine, n],
             dp=at_x(1 if side == 0 else 3),
         )
 
-    def a_next(h):
-        rows = pl.ds(64 * h, 64)
-        slot = abuf.at[mine * 2 + core, rows]
-        return remote(
-            slot, slot, a_ss.at[0, h], a_rs.at[mine, h], dp=at_x(1 + 2 * (r - 2))
-        )
-
-    def a_wait(which, h):
-        slot = abuf.at[which * 2 + core, pl.ds(64 * h, 64)]
-        remote(slot, slot, a_ss.at[0, h], a_rs.at[which, h], dp=at_x(1)).wait_recv()
-
-    @pl.when(r < 2)
-    def _():
-        for h in range(2):
-            a_first(h, 0).start()
-            a_first(h, 1).start()
-        abuf[mine * 2 + core] = bbuf[y]
-
-    @pl.when(r >= 2)
-    def _():
-        for h in range(2):
-            a_wait(mine, h)
-            a_next(h).start()
-
-    twin = dp + 1 - 2 * core
-
-    def x_copy(which):
-        slot = abuf.at[which * 2 + core]
-        return remote(slot, slot, x_ss.at[which], x_rs.at[which], dp=twin)
+    def a_next(n):
+        slot = abuf.at[mine * 2 + core, n]
+        return remote(slot, slot, a_ss.at[0, n], a_rs.at[mine, n], dp=at_x(1 + 2 * (r - 2)))
+
+    def a_wait(which, n):
+        slot = abuf.at[which * 2 + core, n]
+        remote(slot, slot, a_ss.at[0, n], a_rs.at[which, n], dp=at_x(1)).wait_recv()
+
+    def x_copy(which, n):
+        slot = abuf.at[which * 2 + core, n]
+        return remote(slot, slot, x_ss.at[which, n], x_rs.at[which, n], dp=twin)
 
     def x_wait(which):
-        slot = abuf.at[which * 2 + 1 - core]
-        remote(slot, slot, x_ss.at[which], x_rs.at[which], dp=twin).wait_recv()
+        for n in range(CHUNKS):
+            slot = abuf.at[which * 2 + 1 - core, n]
+            remote(slot, slot, x_ss.at[which, n], x_rs.at[which, n], dp=twin).wait_recv()
+
+    scale = 1.0 / jnp.maximum(acc[COLS : COLS + 1, :], 1.0)
+    for n in range(CHUNKS):
+        piece = (acc[WIDE * n : WIDE * (n + 1), :] * scale).T.astype(BF)
+        bbuf[y, n] = piece
+
+        @pl.when(r < 2)
+        def _():
+            a_first(n, 0).start()
+            a_first(n, 1).start()
+            abuf[mine * 2 + core, n] = piece
+            x_copy(mine, n).start()
+
+        b_copy(y, n, 0).start()
+        b_copy(y, n, 1).start()
 
     def c_copy(q, which):
         rows = pl.ds(pl.multiple_of(2 * EX * which, 2 * EX), 2 * EX)
@@ -289,8 +294,10 @@
 
     def block(which, q):
         rows = pl.ds(pl.multiple_of(2 * EX * which, 2 * EX), 2 * EX)
-        a = abuf[pl.ds(which * 2, 2)].reshape(2 * EX, COLS)
-        product = nt(a, bbuf[q]) * (1.0 / R)
+        product = jnp.zeros((2 * EX, EX), F32)
+        for n in range(CHUNKS):
+            product = product + nt(abuf[pl.ds(which * 2, 2), n].reshape(2 * EX, WIDE), bbuf[q, n])
+        product = product * (1.0 / R)
 
         @pl.when(q == zl)
         def _():
@@ -301,26 +308,41 @@
             c_send[q, rows, :] = product.astype(BF)
             c_copy(q, which).start()
 
-    x_copy(mine).start()
-    x_wait(mine)
-    block(mine, y)
-    remote(bbuf.at[before], bbuf.at[before], b_ss.at[0], b_rs.at[0], tensor=ym).wait_recv()
-    b_fwd_up = remote(bbuf.at[before, low], bbuf.at[before, low], b_ss.at[2], b_rs.at[2], tensor=yp)
-    b_fwd_up.start()
-    remote(bbuf.at[after], bbuf.at[after], b_ss.at[1], b_rs.at[1], tensor=yp).wait_recv()
-    b_fwd_down = remote(bbuf.at[after, high], bbuf.at[after, high], b_ss.at[3], b_rs.at[3], tensor=ym)
-    b_fwd_down.start()
+    @pl.when(r < 2)
+    def _():
+        x_wait(mine)
+        block(mine, y)
+
+    for n in range(CHUNKS):
+        @pl.when(r >= 2)
+        def _():
+            a_wait(mine, n)
+            a_next(n).start()
+            x_copy(mine, n).start()
+
+        b_wait(before, n)
+        if n < CHUNKS // 2:
+            b_copy(before, n, 0).start()
+        b_wait(after, n)
+        if n >= CHUNKS // 2:
+            b_copy(after, n, 1).start()
+
+    @pl.when(r >= 2)
+    def _():
+        x_wait(mine)
+        block(mine, y)
+
     block(mine, after)
     block(mine, before)
-    for h in range(2):
-        a_wait(other, h)
-    x_copy(other).start()
+    for n in range(CHUNKS):
+        a_wait(other, n)
+        x_copy(other, n).start()
     x_wait(other)
     block(other, y)
     block(other, after)
     block(other, before)
-    remote(bbuf.at[across, low], bbuf.at[across, low], b_ss.at[2], b_rs.at[2], tensor=ym).wait_recv()
-    remote(bbuf.at[across, high], bbuf.at[across, high], b_ss.at[3], b_rs.at[3], tensor=yp).wait_recv()
+    for n in range(CHUNKS):
+        b_wait(across, n)
     block(mine, across)
     block(other, across)
 
@@ -337,7 +359,7 @@
     out[...] = result
 
     def left(k, c):
-        tok_copy(k).wait_send()
+        tok_copy(k // 8, lax.rem(k, 8)).wait_send()
         return c
 
     lax.fori_loop(1, 32, left, 0)
@@ -348,19 +370,24 @@
             c_copy(lax.rem(zl + k + 1, 4), h).wait_send()
     for h in range(2):
         z_copy(h).wait_send()
-    for cp in (b_up, b_down, b_fwd_up, b_fwd_down, x_copy(0), x_copy(1)):
-        cp.wait_send()
-
-    @pl.when(r < 2)
-    def _():
-        for h in range(2):
-            a_first(h, 0).wait_send()
-            a_first(h, 1).wait_send()
-
-    @pl.when(r >= 2)
-    def _():
-        for h in range(2):
-            a_next(h).wait_send()
+    for n in range(CHUNKS):
+        b_copy(y, n, 0).wait_send()
+        b_copy(y, n, 1).wait_send()
+        if n < CHUNKS // 2:
+            b_copy(before, n, 0).wait_send()
+        else:
+            b_copy(after, n, 1).wait_send()
+        x_copy(0, n).wait_send()
+        x_copy(1, n).wait_send()
+
+        @pl.when(r < 2)
+        def _():
+            a_first(n, 0).wait_send()
+            a_first(n, 1).wait_send()
+
+        @pl.when(r >= 2)
+        def _():
+            a_next(n).wait_send()
 
 
 def body(hidden, out_grad, proj_in, proj_out, owner_ids, example_ids):
@@ -393,14 +420,15 @@
             pltpu.VMEM((COLS + 16, 128 * GROUP), BF),
             pltpu.VMEM((EX, 128 * GROUP), BF),
             pltpu.VMEM((COLS + 16, EX), F32),
-            pltpu.VMEM((4, EX, COLS), BF),
-            pltpu.VMEM((4, EX, COLS), BF),
+            pltpu.VMEM((4, CHUNKS, EX, WIDE), BF),
+            pltpu.VMEM((4, CHUNKS, EX, WIDE), BF),
             pltpu.VMEM((4 * EX, EX), F32),
             pltpu.VMEM((4, 4 * EX, EX), BF),
             pltpu.VMEM((4, 4 * EX, EX), BF),
             dma((4,)), dma((4,)), dma((4,)), dma((3,)), dma((4,)), dma((2,)), dma((2,)),
             dma((2, 4)), dma((2, 4)), dma((32,)), dma((32,)),
-            dma((2, 2)), dma((2, 2)), dma((2,)), dma((2,)), dma((4,)), dma((4,)), dma((4, 2)), dma((4, 2)),
+            dma((2, CHUNKS)), dma((2, CHUNKS)), dma((2, CHUNKS)), dma((2, CHUNKS)),
+            dma((4, CHUNKS, 2)), dma((4, CHUNKS)), dma((4, 2)), dma((4, 2)),
         ],
         compiler_params=pltpu.CompilerParams(
             collective_id=0, has_side_effects=True, vmem_limit_bytes=60 * 1024 * 1024

time: 70.3 us -> 68.8 us (0.979)
  Pallas kernels: 68.5 us -> 67 us
    pallas_call x1, Pallas kernels: 68.5 us -> 67 us  [body(): pl.pallas_call(kernel, out_shape=jax.ShapeDtypeStruct((4 * EX, EX), F32),...]
where the time goes in v3:
time: 68.8 us; the launch traced here: 68.7 us
  Pallas kernels  67 us (97%)
  local copies, waits for them, and re-layouts  1.67 us (2%)
    pallas_call x1, Pallas kernels, body(): pl.pallas_call(kernel, out_shape=jax.ShapeDtypeStruct((4 * EX, EX), F32),...  67 us
    unnamed x1, local copies, waits for them, and re-layouts  1.67 us

profile of v3, /device:TPU:21, one launch (start us, length us, event | category | flops | bytes accessed | tf_op | source)
XLA Modules:
  0.0 68.7 jit_solution(18339549219514700965)
XLA Ops:
  0.0 67.0 %per_example_kernel.1 = f32[512,128]{1,0:T(8,128)} custom-call(bf16[1024,3584]{1,0:T(8,128)(2,1)} %hid.1, bf16[1024,1024]{1,0:T(8,128)(2,1)} %og.1, bf16[64,3584]{1,0:T(8,128)(2,1)} %bitcast.4, bf16[64,1024]{1,0:T(8,128)(2,1)} %bitcast.5, s32[1,1024]{1,0:T(1,128)} %bitcast.6, s32[1,1024]{1,0:T(1,128)} %bitcast.7), custom_call_target="tpu_custom_call" | custom-call | tf_op jit(solution)/shard_map/per_example_kernel/pallas_call | solution.py:398
  67.0 1.7 %copy.8 = f32[512,128]{1,0:T(8,128)} copy(f32[512,128]{1,0:T(8,128)} %per_example_kernel.1) | data formatting | bytes 524288

commit v4 on v3

--- a/solution.py
+++ b/solution.py
@@ -28,8 +28,8 @@
     hid, og, pin, pout, own_in, exi_in, out,
     own, exi,
     hbuf, gbuf, pinb, poutb, part_own, rs_send, rs_recv, z_send, z_recv, vals, slots,
-    routed, sbuf, rbuf, outer, member, acc, bbuf, abuf, keep, c_send, c_recv,
-    hsem, gsem, psem, rs_ss, rs_rs, z_ss, z_rs, v_ss, v_rs, t_ss, t_rs,
+    routed, ids_send, ids_recv, sbuf, rbuf, outer, member, acc, bbuf, abuf, keep, sums, c_send, c_recv,
+    hsem, gsem, psem, rs_ss, rs_rs, z_ss, z_rs, v_ss, v_rs, i_ss, i_rs, t_ss, t_rs,
     a_ss, a_rs, x_ss, x_rs, b_ss, b_rs, c_ss, c_rs,
 ):
     dp = lax.axis_index("dp")
@@ -104,14 +104,15 @@
         hit = key == lax.broadcasted_iota(jnp.int32, (128, TOK), 0) + 128 * o
         slots[128 * o : 128 * (o + 1), :] = hit.astype(F32).astype(BF)
         ids = nt(idrow, slots[128 * o : 128 * (o + 1), :])[0:8, :].astype(BF)
-        for q in range(4):
-            sbuf[o, q, R : R + 8, :] = ids
+        ids_send[o] = ids
     outer[COLS : COLS + 16, :] = jnp.ones((16, 128 * GROUP), BF)
     acc[...] = jnp.zeros_like(acc)
 
-    def rs_copy(k):
+    def rs_copy(k, ch):
         p = lax.rem(y + 1 + k, 4)
-        return remote(rs_send.at[k], rs_recv.at[y], rs_ss.at[k], rs_rs.at[y], tensor=p * 2 + zh)
+        return remote(
+            rs_send.at[k, ch], rs_recv.at[y, ch], rs_ss.at[k, ch], rs_rs.at[y, ch], tensor=p * 2 + zh
+        )
 
     def project(k):
         p = lax.rem(y + 1 + k, 4)
@@ -123,33 +124,48 @@
 
     cp_out.wait()
     cp_in.wait()
+    xc = lax.rem(dp, 8)
+
+    def ids_copy(dz, j):
+        zq, xq = lax.rem(zl + dz, 4), lax.rem(xc + j, 8)
+        return remote(
+            ids_send.at[xq], ids_recv.at[dp], i_ss.at[dz * 8 + j], i_rs.at[dp], dp=zq * 8 + xq
+        )
+
+    def ids_start(k, c):
+        ids_copy(k // 8, lax.rem(k, 8)).start()
+        return c
+
     for k in range(3):
         both = project(k).astype(BF)
         rs_send[k, 0] = both[:, :128]
         rs_send[k, 1] = both[:, 128:]
         if k == 0:
             pl.semaphore_wait(barrier, 35)
-        rs_copy(k).start()
+        rs_copy(k, 0).start()
+        rs_copy(k, 1).start()
     both = project(3)
     part_own[0] = both[:, :128]
     part_own[1] = both[:, 128:]
 
-    for k in range(1, 4):
-        src = lax.rem(y + k, 4)
-        remote(
-            rs_send.at[0], rs_recv.at[src], rs_ss.at[0], rs_rs.at[src], tensor=src * 2 + zh
-        ).wait_recv()
-
     def z_copy(ch):
         return remote(z_send.at[ch], z_recv.at[ch], z_ss.at[ch], z_rs.at[ch], tensor=y * 2 + 1 - zh)
 
     for ch in range(2):
         total = part_own[ch]
         for k in range(1, 4):
-            total = total + rs_recv[lax.rem(y + k, 4), ch].astype(F32)
+            src = lax.rem(y + k, 4)
+            remote(
+                rs_send.at[0, ch], rs_recv.at[src, ch], rs_ss.at[0, ch], rs_rs.at[src, ch],
+                tensor=src * 2 + zh,
+            ).wait_recv()
+            total = total + rs_recv[src, ch].astype(F32)
         z_send[ch] = total.astype(BF)
         z_copy(ch).start()
         part_own[ch] = total
+
+    lax.fori_loop(1, 32, ids_start, 0)
+    ids_recv[dp] = ids_send[xc]
 
     def v_copy(ch, k):
         return remote(vals.at[ch, y], vals.at[ch, y], v_ss.at[ch, k], v_rs.at[ch, y], tensor=at_y(k))
@@ -180,7 +196,6 @@
                     sbuf[4 * b + o, q, 0:HALF, :] = piece[HALF * (q // 2) : HALF * (q // 2 + 1), :]
                     sbuf[4 * b + o, q, HALF:R, :] = piece[R + HALF * (q % 2) : R + HALF * (q % 2 + 1), :]
 
-    xc = lax.rem(dp, 8)
 
     def tok_copy(dz, j):
         zq, xq = lax.rem(zl + dz, 4), lax.rem(xc + j, 8)
@@ -195,7 +210,7 @@
 
         lax.fori_loop(1 if dz == 0 else 0, 8, step, 0)
 
-    for dz in (2, 1, 3, 0):
+    for dz in (1, 3, 2, 0):
         tok_start(dz)
     rbuf[dp] = sbuf[xc, zl]
 
@@ -207,6 +222,9 @@
             src = lax.rem(zl + 4 - dz, 4) * 8 + lax.rem(xc + 8 - j, 8)
 
             def arrived():
+                remote(
+                    ids_send.at[0], ids_recv.at[src], i_ss.at[0], i_rs.at[src], dp=src
+                ).wait_recv()
                 remote(
                     sbuf.at[0, 0], rbuf.at[src], t_ss.at[0], t_rs.at[src], dp=src
                 ).wait_recv()
@@ -220,7 +238,7 @@
             lanes = slice(128 * s, 128 * (s + 1))
             for i in range(HALF):
                 outer[HALF * i : HALF * (i + 1), lanes] = (xr[i : i + 1, :] * gr).astype(BF)
-            ids = rbuf[src, R : R + 8, :].astype(F32)[0:1, :].astype(jnp.int32)
+            ids = ids_recv[src].astype(F32)[0:1, :].astype(jnp.int32)
             member[:, lanes] = (
                 (ids == lax.broadcasted_iota(jnp.int32, (EX, 128), 0) + 1).astype(F32).astype(BF)
             )
@@ -265,10 +283,9 @@
         slot = abuf.at[which * 2 + core, n]
         return remote(slot, slot, x_ss.at[which, n], x_rs.at[which, n], dp=twin)
 
-    def x_wait(which):
-        for n in range(CHUNKS):
-            slot = abuf.at[which * 2 + 1 - core, n]
-            remote(slot, slot, x_ss.at[which, n], x_rs.at[which, n], dp=twin).wait_recv()
+    def x_wait(which, n):
+        slot = abuf.at[which * 2 + 1 - core, n]
+        remote(slot, slot, x_ss.at[which, n], x_rs.at[which, n], dp=twin).wait_recv()
 
     scale = 1.0 / jnp.maximum(acc[COLS : COLS + 1, :], 1.0)
     for n in range(CHUNKS):
@@ -292,11 +309,13 @@
             dp=q * 8 + x * 2 + core,
         )
 
-    def block(which, q):
+    def term(which, q, n):
+        return nt(abuf[pl.ds(which * 2, 2), n].reshape(2 * EX, WIDE), bbuf[q, n])
+
+    def block(which, q, product=None, begin=0):
         rows = pl.ds(pl.multiple_of(2 * EX * which, 2 * EX), 2 * EX)
-        product = jnp.zeros((2 * EX, EX), F32)
-        for n in range(CHUNKS):
-            product = product + nt(abuf[pl.ds(which * 2, 2), n].reshape(2 * EX, WIDE), bbuf[q, n])
+        for n in range(begin, CHUNKS):
+            product = term(which, q, n) if product is None else product + term(which, q, n)
         product = product * (1.0 / R)
 
         @pl.when(q == zl)
@@ -310,7 +329,8 @@
 
     @pl.when(r < 2)
     def _():
-        x_wait(mine)
+        for n in range(CHUNKS):
+            x_wait(mine, n)
         block(mine, y)
 
     for n in range(CHUNKS):
@@ -329,42 +349,50 @@
 
     @pl.when(r >= 2)
     def _():
-        x_wait(mine)
+        for n in range(CHUNKS):
+            x_wait(mine, n)
         block(mine, y)
 
     block(mine, after)
     block(mine, before)
+    near = (y, after, before)
     for n in range(CHUNKS):
         a_wait(other, n)
         x_copy(other, n).start()
-    x_wait(other)
-    block(other, y)
-    block(other, after)
-    block(other, before)
+        if n > 0:
+            x_wait(other, n - 1)
+            for t in range(3):
+                new = term(other, near[t], n - 1)
+                sums[t] = new if n == 1 else sums[t] + new
     for n in range(CHUNKS):
         b_wait(across, n)
     block(mine, across)
+    x_wait(other, CHUNKS - 1)
+    for t in range(3):
+        block(other, near[t], sums[t], CHUNKS - 1)
     block(other, across)
 
-    result = keep[...]
-    for k in range(1, 4):
-        src = lax.rem(zl + k, 4)
-        for which in range(2):
-            rows = slice(2 * EX * which, 2 * EX * (which + 1))
+    for which in range(2):
+        rows = slice(2 * EX * which, 2 * EX * (which + 1))
+        result = keep[rows, :]
+        for k in range(1, 4):
+            src = lax.rem(zl + k, 4)
             remote(
                 c_send.at[src, rows], c_recv.at[src, rows], c_ss.at[src, which], c_rs.at[src, which],
                 dp=src * 8 + x * 2 + core,
             ).wait_recv()
-        result = result + c_recv[src].astype(F32)
-    out[...] = result
+            result = result + c_recv[src, rows, :].astype(F32)
+        out[rows, :] = result
 
     def left(k, c):
         tok_copy(k // 8, lax.rem(k, 8)).wait_send()
+        ids_copy(k // 8, lax.rem(k, 8)).wait_send()
         return c
 
     lax.fori_loop(1, 32, left, 0)
     for k in range(3):
-        rs_copy(k).wait_send()
+        rs_copy(k, 0).wait_send()
+        rs_copy(k, 1).wait_send()
         for h in range(2):
             v_copy(h, k + 1).wait_send()
             c_copy(lax.rem(zl + k + 1, 4), h).wait_send()
@@ -415,18 +443,21 @@
             pltpu.VMEM((2, 4, 2 * R, 128), BF),
             pltpu.VMEM((8 * 128, TOK), BF),
             pltpu.VMEM((2 * R, 8 * 128), F32),
-            pltpu.VMEM((8, 4, R + 8, 128), BF),
-            pltpu.VMEM((32, R + 8, 128), BF),
+            pltpu.VMEM((8, 8, 128), BF),
+            pltpu.VMEM((32, 8, 128), BF),
+            pltpu.VMEM((8, 4, R, 128), BF),
+            pltpu.VMEM((32, R, 128), BF),
             pltpu.VMEM((COLS + 16, 128 * GROUP), BF),
             pltpu.VMEM((EX, 128 * GROUP), BF),
             pltpu.VMEM((COLS + 16, EX), F32),
             pltpu.VMEM((4, CHUNKS, EX, WIDE), BF),
             pltpu.VMEM((4, CHUNKS, EX, WIDE), BF),
             pltpu.VMEM((4 * EX, EX), F32),
+            pltpu.VMEM((3, 2 * EX, EX), F32),
             pltpu.VMEM((4, 4 * EX, EX), BF),
             pltpu.VMEM((4, 4 * EX, EX), BF),
-            dma((4,)), dma((4,)), dma((4,)), dma((3,)), dma((4,)), dma((2,)), dma((2,)),
-            dma((2, 4)), dma((2, 4)), dma((32,)), dma((32,)),
+            dma((4,)), dma((4,)), dma((4,)), dma((3, 2)), dma((4, 2)), dma((2,)), dma((2,)),
+            dma((2, 4)), dma((2, 4)), dma((32,)), dma((32,)), dma((32,)), dma((32,)),
             dma((2, CHUNKS)), dma((2, CHUNKS)), dma((2, CHUNKS)), dma((2, CHUNKS)),
             dma((4, CHUNKS, 2)), dma((4, CHUNKS)), dma((4, 2)), dma((4, 2)),
         ],

time: 68.8 us -> 67 us (0.974)
  Pallas kernels: 67 us -> 64.9 us
    pallas_call x1, Pallas kernels: 67 us -> 64.9 us  [body(): pl.pallas_call(kernel, out_shape=jax.ShapeDtypeStruct((4 * EX, EX), F32),...]
where the time goes in v4:
time: 67 us; the launch traced here: 66.6 us
  Pallas kernels  64.9 us (97%)
  local copies, waits for them, and re-layouts  1.67 us (2%)
    pallas_call x1, Pallas kernels, body(): pl.pallas_call(kernel, out_shape=jax.ShapeDtypeStruct((4 * EX, EX), F32),...  64.9 us
    unnamed x1, local copies, waits for them, and re-layouts  1.67 us

profile of v4, /device:TPU:21, one launch (start us, length us, event | category | flops | bytes accessed | tf_op | source)
XLA Modules:
  0.0 66.6 jit_solution(4269197105507942514)
XLA Ops:
  0.0 64.9 %per_example_kernel.1 = f32[512,128]{1,0:T(8,128)} custom-call(bf16[1024,3584]{1,0:T(8,128)(2,1)} %hid.1, bf16[1024,1024]{1,0:T(8,128)(2,1)} %og.1, bf16[64,3584]{1,0:T(8,128)(2,1)} %bitcast.4, bf16[64,1024]{1,0:T(8,128)(2,1)} %bitcast.5, s32[1,1024]{1,0:T(1,128)} %bitcast.6, s32[1,1024]{1,0:T(1,128)} %bitcast.7), custom_call_target="tpu_custom_call" | custom-call | tf_op jit(solution)/shard_map/per_example_kernel/pallas_call | solution.py:426
  64.9 1.7 %copy.8 = f32[512,128]{1,0:T(8,128)} copy(f32[512,128]{1,0:T(8,128)} %per_example_kernel.1) | data formatting | bytes 524288

commit v5 on v4

--- a/solution.py
+++ b/solution.py
@@ -336,9 +336,10 @@
     for n in range(CHUNKS):
         @pl.when(r >= 2)
         def _():
-            a_wait(mine, n)
-            a_next(n).start()
-            x_copy(mine, n).start()
+            for m in ((0, 1, 2, 3), (), (), ())[n]:
+                a_wait(mine, m)
+                a_next(m).start()
+                x_copy(mine, m).start()
 
         b_wait(before, n)
         if n < CHUNKS // 2:
@@ -363,14 +364,18 @@
             x_wait(other, n - 1)
             for t in range(3):
                 new = term(other, near[t], n - 1)
-                sums[t] = new if n == 1 else sums[t] + new
+                sums[near[t]] = new if n == 1 else sums[near[t]] + new
     for n in range(CHUNKS):
         b_wait(across, n)
     block(mine, across)
+    partial = term(other, across, 0)
+    for n in range(1, CHUNKS - 1):
+        partial = partial + term(other, across, n)
+    sums[across] = partial
     x_wait(other, CHUNKS - 1)
-    for t in range(3):
-        block(other, near[t], sums[t], CHUNKS - 1)
-    block(other, across)
+    for k in (2, 1, 3, 0):
+        q = lax.rem(zl + k, 4)
+        block(other, q, sums[q], CHUNKS - 1)
 
     for which in range(2):
         rows = slice(2 * EX * which, 2 * EX * (which + 1))
@@ -453,7 +458,7 @@
             pltpu.VMEM((4, CHUNKS, EX, WIDE), BF),
             pltpu.VMEM((4, CHUNKS, EX, WIDE), BF),
             pltpu.VMEM((4 * EX, EX), F32),
-            pltpu.VMEM((3, 2 * EX, EX), F32),
+            pltpu.VMEM((4, 2 * EX, EX), F32),
             pltpu.VMEM((4, 4 * EX, EX), BF),
             pltpu.VMEM((4, 4 * EX, EX), BF),
             dma((4,)), dma((4,)), dma((4,)), dma((3, 2)), dma((4, 2)), dma((2,)), dma((2,)),

time: 67 us -> 66.5 us (level); the launches traced: 66.6 us -> 65.4 us
  Pallas kernels: 64.9 us -> 63.7 us
    pallas_call x1, Pallas kernels: 64.9 us -> 63.7 us  [body(): pl.pallas_call(kernel, out_shape=jax.ShapeDtypeStruct((4 * EX, EX), F32),...]
where the time goes in v5:
time: 66.5 us; the launch traced here: 65.4 us
  Pallas kernels  63.7 us (96%)
  local copies, waits for them, and re-layouts  1.67 us (3%)
    pallas_call x1, Pallas kernels, body(): pl.pallas_call(kernel, out_shape=jax.ShapeDtypeStruct((4 * EX, EX), F32),...  63.7 us
    unnamed x1, local copies, waits for them, and re-layouts  1.67 us

profile of v5, /device:TPU:21, one launch (start us, length us, event | category | flops | bytes accessed | tf_op | source)
XLA Modules:
  0.0 65.4 jit_solution(9249944349402851472)
XLA Ops:
  0.0 63.7 %per_example_kernel.1 = f32[512,128]{1,0:T(8,128)} custom-call(bf16[1024,3584]{1,0:T(8,128)(2,1)} %hid.1, bf16[1024,1024]{1,0:T(8,128)(2,1)} %og.1, bf16[64,3584]{1,0:T(8,128)(2,1)} %bitcast.4, bf16[64,1024]{1,0:T(8,128)(2,1)} %bitcast.5, s32[1,1024]{1,0:T(1,128)} %bitcast.6, s32[1,1024]{1,0:T(1,128)} %bitcast.7), custom_call_target="tpu_custom_call" | custom-call | tf_op jit(solution)/shard_map/per_example_kernel/pallas_call | solution.py:431
  63.7 1.7 %copy.8 = f32[512,128]{1,0:T(8,128)} copy(f32[512,128]{1,0:T(8,128)} %per_example_kernel.1) | data formatting | bytes 524288

commit v6 on v5

--- a/solution.py
+++ b/solution.py
@@ -80,6 +80,46 @@
     for k in range(1, 4):
         pl.semaphore_signal(barrier, inc=1, device_id={"tensor": at_y(k)}, device_id_type=MESH)
     pl.semaphore_signal(barrier, inc=1, device_id={"tensor": y * 2 + 1 - zh}, device_id_type=MESH)
+
+    def rs_copy(k, ch):
+        p = lax.rem(y + 1 + k, 4)
+        return remote(
+            rs_send.at[k, ch], rs_recv.at[y, ch], rs_ss.at[k, ch], rs_rs.at[y, ch], tensor=p * 2 + zh
+        )
+
+    def project(k):
+        p = lax.rem(y + 1 + k, 4)
+        for cp in load(k):
+            cp.wait()
+        gp = nt(gbuf[p], poutb[...])
+        xp = nt(hbuf[p], pinb[...])
+        return jnp.concatenate([xp, gp], 1).T
+
+    cp_out.wait()
+    cp_in.wait()
+    xc = lax.rem(dp, 8)
+
+    def ids_copy(dz, j):
+        zq, xq = lax.rem(zl + dz, 4), lax.rem(xc + j, 8)
+        return remote(
+            ids_send.at[xq], ids_recv.at[dp], i_ss.at[dz * 8 + j], i_rs.at[dp], dp=zq * 8 + xq
+        )
+
+    def ids_start(k, c):
+        ids_copy(k // 8, lax.rem(k, 8)).start()
+        return c
+
+    for k in range(3):
+        both = project(k).astype(BF)
+        rs_send[k, 0] = both[:, :128]
+        rs_send[k, 1] = both[:, 128:]
+        if k == 0:
+            pl.semaphore_wait(barrier, 35)
+        rs_copy(k, 0).start()
+        rs_copy(k, 1).start()
+    both = project(3)
+    part_own[0] = both[:, :128]
+    part_own[1] = both[:, 128:]
 
     cp_own.wait()
     cp_exi.wait()
@@ -107,46 +147,6 @@
         ids_send[o] = ids
     outer[COLS : COLS + 16, :] = jnp.ones((16, 128 * GROUP), BF)
     acc[...] = jnp.zeros_like(acc)
-
-    def rs_copy(k, ch):
-        p = lax.rem(y + 1 + k, 4)
-        return remote(
-            rs_send.at[k, ch], rs_recv.at[y, ch], rs_ss.at[k, ch], rs_rs.at[y, ch], tensor=p * 2 + zh
-        )
-
-    def project(k):
-        p = lax.rem(y + 1 + k, 4)
-        for cp in load(k):
-            cp.wait()
-        gp = nt(gbuf[p], poutb[...])
-        xp = nt(hbuf[p], pinb[...])
-        return jnp.concatenate([xp, gp], 1).T
-
-    cp_out.wait()
-    cp_in.wait()
-    xc = lax.rem(dp, 8)
-
-    def ids_copy(dz, j):
-        zq, xq = lax.rem(zl + dz, 4), lax.rem(xc + j, 8)
-        return remote(
-            ids_send.at[xq], ids_recv.at[dp], i_ss.at[dz * 8 + j], i_rs.at[dp], dp=zq * 8 + xq
-        )
-
-    def ids_start(k, c):
-        ids_copy(k // 8, lax.rem(k, 8)).start()
-        return c
-
-    for k in range(3):
-        both = project(k).astype(BF)
-        rs_send[k, 0] = both[:, :128]
-        rs_send[k, 1] = both[:, 128:]
-        if k == 0:
-            pl.semaphore_wait(barrier, 35)
-        rs_copy(k, 0).start()
-        rs_copy(k, 1).start()
-    both = project(3)
-    part_own[0] = both[:, :128]
-    part_own[1] = both[:, 128:]
 
     def z_copy(ch):
         return remote(z_send.at[ch], z_recv.at[ch], z_ss.at[ch], z_rs.at[ch], tensor=y * 2 + 1 - zh)

time: 66.5 us -> 66.6 us (level)
  the two profiles are of different devices: /device:TPU:21 before, /device:TPU:71 now
where the time goes in v6:
time: 66.6 us; the launch traced here: 66.5 us
  Pallas kernels  64.8 us (97%)
  local copies, waits for them, and re-layouts  1.67 us (3%)
    pallas_call x1, Pallas kernels, body(): pl.pallas_call(kernel, out_shape=jax.ShapeDtypeStruct((4 * EX, EX), F32),...  64.8 us
    unnamed x1, local copies, waits for them, and re-layouts  1.67 us

profile of v6, /device:TPU:71, one launch (start us, length us, event | category | flops | bytes accessed | tf_op | source)
XLA Modules:
  0.0 66.5 jit_solution(16701250699163848940)
XLA Ops:
  0.0 64.8 %per_example_kernel.1 = f32[512,128]{1,0:T(8,128)} custom-call(bf16[1024,3584]{1,0:T(8,128)(2,1)} %hid.1, bf16[1024,1024]{1,0:T(8,128)(2,1)} %og.1, bf16[64,3584]{1,0:T(8,128)(2,1)} %bitcast.4, bf16[64,1024]{1,0:T(8,128)(2,1)} %bitcast.5, s32[1,1024]{1,0:T(1,128)} %bitcast.6, s32[1,1024]{1,0:T(1,128)} %bitcast.7), custom_call_target="tpu_custom_call" | custom-call | tf_op jit(solution)/shard_map/per_example_kernel/pallas_call | solution.py:431
  64.8 1.7 %copy.8 = f32[512,128]{1,0:T(8,128)} copy(f32[512,128]{1,0:T(8,128)} %per_example_kernel.1) | data formatting | bytes 524288
